TPU v7x, 32 devices: a whole 2x2x4 slice. The times are simulated.
32 devices in a mesh: groups: 2 (over x), sensor: 16 (over z, y, core).
Axes of the slice: x: 2, y: 2, z: 4, core: 2. Of those that a mesh axis runs over, the one named last changes fastest.
Arguments:
- series: float32 [288, 1536], P(None, ('groups', 'sensor')), parts along dimension 1, may hold values from -6 to 6
- starts: int32 [2], P('groups'), parts along dimension 0, may hold values from 0 to 276
- sensor_order: int32 [1536], P(('groups', 'sensor')), parts along dimension 0, may hold values from 0 to 767, each once
- emb_src: float32 [10, 1536], P(None, ('groups', 'sensor')), parts along dimension 1, may hold values from -4.4 to 330
- emb_dst: float32 [10, 1536], P(None, ('groups', 'sensor')), parts along dimension 1, may hold values from -4.4 to 4.4
- start_proj: float32 [2, 32], replicated, may hold values from -4 to 4
- conv_weight: bfloat16 [64, 64], replicated, may hold values from -0.75 to 0.75
- mix_weight: bfloat16 [96, 32], replicated, may hold values from -0.625 to 0.625
- out_grad: bfloat16 [1536, 384], P(('groups', 'sensor')), parts along dimension 0, may hold values from -0.59765625 to 0.59765625
Outputs:
- layer_out: bfloat16 [1536, 384], P(('groups', 'sensor')), parts along dimension 0
- grad_src: float32 [10, 1536], P(None, ('groups', 'sensor')), parts along dimension 1
- grad_dst: float32 [10, 1536], P(None, ('groups', 'sensor')), parts along dimension 1
- grad_mix: float32 [192, 32], P('groups'), parts along dimension 0
There are 2 independent parts, one for each index of `groups`. A program takes and returns all parts, laid end to end along the dimension named above; an argument that names none is the same for every part. Nothing has to cross between parts.
All inputs are finite; a program needn't handle non-finite values.
Results may differ from a plain program's by a relative error of at most 0.035.
Values may be sent and summed in bfloat16 or wider, within the bound.
A program may use at most 64 MiB of HBM per device.

v0:
```python
import math
import jax
import jax.numpy as jnp
from jax import lax
from jax.sharding import PartitionSpec as P

STEPS = 12
highest = lax.Precision.HIGHEST


def front(readings, start_proj, conv_weight):
    sensors_here = readings.shape[0]
    channels = start_proj.shape[1]
    padded = jnp.concatenate(
        [jnp.zeros(readings.shape[:-1] + (1,), jnp.float32), readings], axis=-1
    )
    inputs = (padded[..., None] * start_proj[0] + start_proj[1]).astype(jnp.bfloat16)
    paired = jnp.concatenate([inputs[:, :, :-1, :], inputs[:, :, 1:, :]], axis=-1).reshape(
        -1, 2 * channels
    )
    gate_terms = jnp.dot(paired, conv_weight, preferred_element_type=jnp.float32)
    hidden = (jnp.tanh(gate_terms[:, :channels]) * jax.nn.sigmoid(gate_terms[:, channels:])).astype(
        jnp.bfloat16
    )
    return (hidden.reshape(sensors_here, -1), inputs[:, :, 1:, :].reshape(sensors_here, -1))


def mixing(residual, hidden, diffused, second, mix_weight):
    channels = mix_weight.shape[1]
    stacked = jnp.concatenate(
        [member.reshape(-1, channels) for member in (hidden, diffused, second)], axis=1
    )
    summed = residual.reshape(-1, channels).astype(jnp.float32) + jnp.dot(
        stacked, mix_weight, preferred_element_type=jnp.float32
    )
    return (summed.astype(jnp.bfloat16).reshape(hidden.shape[0], -1), stacked)


def channel_grads(out_grad, mix_weight):
    channels = mix_weight.shape[1]
    row_count = out_grad.shape[0]
    flat_grad = out_grad.reshape(-1, channels)
    dims = (((1,), (1,)), ((), ()))
    grad_once = lax.dot_general(
        flat_grad, mix_weight[channels : 2 * channels], dims, preferred_element_type=jnp.float32
    )
    grad_twice = lax.dot_general(
        flat_grad, mix_weight[2 * channels :], dims, preferred_element_type=jnp.float32
    )
    return (
        grad_once.astype(jnp.bfloat16).reshape(row_count, -1),
        grad_twice.astype(jnp.bfloat16).reshape(row_count, -1),
    )


def tile_probs(rows_emb, cols_emb, row_max, row_total):
    scores = jnp.einsum("ei,ej->ij", rows_emb, cols_emb, precision=highest)
    shares = jnp.exp(jnp.maximum(scores, 0.0) - row_max[:, None]) / row_total[:, None]
    return (scores, shares)


def pair_dot(left, right):
    return lax.dot_general(
        left, right, (((1,), (1,)), ((), ())), preferred_element_type=jnp.float32
    )


def in_blocks(step_fn, status, members, axis_dim):
    amount = members[0].shape[axis_dim]
    span_size = math.gcd(amount, 512)

    def advance(position, current):
        opening = position * span_size
        sliced = tuple(
            (lax.dynamic_slice_in_dim(member, opening, span_size, axis_dim) for member in members)
        )
        return step_fn(current, sliced, opening)

    return lax.fori_loop(0, amount // span_size, advance, status)


def score_grads(status, emb_src, cols_dst, offset, scores, shares, dweights):
    grad_rows, grad_cols = status
    dscore = jnp.where(scores > 0.0, shares * dweights, 0.0)
    grad_rows = grad_rows + jnp.einsum("ej,ij->ei", cols_dst, dscore, precision=highest)
    span_size = dscore.shape[1]
    current = lax.dynamic_slice_in_dim(grad_cols, offset, span_size, 1)
    added = current + jnp.einsum("ei,ij->ej", emb_src, dscore, precision=highest)
    return (grad_rows, lax.dynamic_update_slice_in_dim(grad_cols, added, offset, 1))


def per_device(
    series, starts, sensor_order, emb_src, emb_dst, start_proj, conv_weight, mix_weight, out_grad
):
    local_rows = sensor_order.shape[0]
    embed_dim = emb_src.shape[0]
    channels = start_proj.shape[1]
    all_rows = local_rows * lax.axis_size("sensor")
    windows = jax.vmap(lambda first_step: lax.dynamic_slice_in_dim(series, first_step, STEPS, 0))(
        starts
    )
    flat_windows = windows.reshape(-1, local_rows)
    window_rows = flat_windows.shape[0]

    def pick_step(status, members, offset):
        readings_sum, dst_all = status
        block_windows, block_dst = members
        span_size = block_windows.shape[1]
        onehot = (sensor_order[:, None] == offset + lax.iota(jnp.int32, span_size)[None, :]).astype(
            jnp.float32
        )
        readings_sum = readings_sum + jnp.einsum(
            "wj,pj->wp", block_windows, onehot, precision=highest
        )
        return (readings_sum, lax.dynamic_update_slice_in_dim(dst_all, block_dst, offset, 1))

    readings_sum, dst_all = in_blocks(
        pick_step,
        (
            jnp.zeros((window_rows, local_rows), jnp.float32),
            jnp.zeros((embed_dim, all_rows), jnp.float32),
        ),
        (
            lax.all_gather(flat_windows, "sensor", axis=1, tiled=True),
            lax.all_gather(emb_dst, "sensor", axis=1, tiled=True),
        ),
        1,
    )
    readings = readings_sum.T.reshape(local_rows, -1, STEPS)
    hidden, residual = front(readings, start_proj, conv_weight)
    feat_cols = hidden.shape[1]
    span_all = math.gcd(all_rows, 512)

    def stat_step(position, current):
        best_score, summed = current
        cols_dst = lax.dynamic_slice_in_dim(dst_all, position * span_all, span_all, 1)
        scores = jnp.maximum(jnp.einsum("ei,ej->ij", emb_src, cols_dst, precision=highest), 0.0)
        new_best = jnp.maximum(best_score, jnp.max(scores, axis=1))
        summed = summed * jnp.exp(best_score - new_best) + jnp.sum(
            jnp.exp(scores - new_best[:, None]), axis=1
        )
        return (new_best, summed)

    row_max, row_total = lax.fori_loop(
        0,
        all_rows // span_all,
        stat_step,
        (jnp.zeros((local_rows,), jnp.float32), jnp.zeros((local_rows,), jnp.float32)),
    )
    grad_once, grad_twice = channel_grads(out_grad, mix_weight)

    def spread_step(status, members, offset):
        block_feat = members[0]
        cols_dst = lax.dynamic_slice_in_dim(dst_all, offset, block_feat.shape[0], 1)
        scores, shares = tile_probs(emb_src, cols_dst, row_max, row_total)
        return status + jnp.dot(
            shares.astype(jnp.bfloat16), block_feat, preferred_element_type=jnp.float32
        )

    first_init = jnp.zeros((local_rows, feat_cols), jnp.float32)
    first_result = in_blocks(
        spread_step, first_init, (lax.all_gather(hidden, "sensor", axis=0, tiled=True),), 0
    )
    diffused = first_result.astype(jnp.bfloat16)

    def plain_step(status, members, offset):
        accumulated, grad_rows, grad_cols = status
        return (spread_step(accumulated, members, offset), grad_rows, grad_cols)

    second_init = (
        jnp.zeros((local_rows, feat_cols), jnp.float32),
        jnp.zeros((embed_dim, local_rows), jnp.float32),
        jnp.zeros((embed_dim, all_rows), jnp.float32),
    )
    second_result = in_blocks(
        plain_step, second_init, (lax.all_gather(diffused, "sensor", axis=0, tiled=True),), 0
    )
    second_full, grad_rows, grad_cols = second_result
    second = second_full.astype(jnp.bfloat16)
    layer_out, stacked = mixing(residual, hidden, diffused, second, mix_weight)
    mix_part = lax.dot_general(
        stacked,
        out_grad.reshape(-1, channels),
        (((0,), (0,)), ((), ())),
        preferred_element_type=jnp.float32,
    )
    span_size = math.gcd(lax.axis_size("sensor") * local_rows, 512)

    def piece_term(position):
        cols_dst = lax.dynamic_slice_in_dim(dst_all, position * span_size, span_size, 1)
        scores, shares = tile_probs(emb_src, cols_dst, row_max, row_total)
        return lax.dot_general(
            shares.astype(jnp.bfloat16),
            grad_twice,
            (((0,), (0,)), ((), ())),
            preferred_element_type=jnp.float32,
        )

    adjoint_sum = lax.psum_scatter(
        lax.map(
            piece_term,
            jnp.arange(lax.axis_size("sensor") * local_rows // span_size, dtype=jnp.int32),
        ).reshape(lax.axis_size("sensor") * local_rows, -1),
        "sensor",
        scatter_dimension=0,
        tiled=True,
    )
    carried = (grad_once.astype(jnp.float32) + adjoint_sum).astype(jnp.bfloat16)
    row_delta = jnp.sum(
        grad_twice.astype(jnp.float32) * second_full + carried.astype(jnp.float32) * first_result,
        axis=1,
    )

    def pair_step(status, members, offset):
        block_hidden, block_diff = members
        cols_dst = lax.dynamic_slice_in_dim(dst_all, offset, block_hidden.shape[0], 1)
        scores, shares = tile_probs(emb_src, cols_dst, row_max, row_total)
        dweights = (
            pair_dot(grad_twice, block_diff) + pair_dot(carried, block_hidden) - row_delta[:, None]
        )
        return score_grads(status, emb_src, cols_dst, offset, scores, shares, dweights)

    grad_rows, grad_cols = in_blocks(
        pair_step,
        (grad_rows, grad_cols),
        (
            lax.all_gather(hidden, "sensor", axis=0, tiled=True),
            lax.all_gather(diffused, "sensor", axis=0, tiled=True),
        ),
        0,
    )
    grad_dst = lax.psum_scatter(grad_cols, "sensor", scatter_dimension=1, tiled=True)
    grad_mix = lax.psum(mix_part, "sensor")
    return (layer_out, grad_rows, grad_dst, grad_mix)


def solution(mesh):
    placed = (
        P(None, ("groups", "sensor")),
        P("groups"),
        P(("groups", "sensor")),
        P(None, ("groups", "sensor")),
        P(None, ("groups", "sensor")),
        P(),
        P(),
        P(),
        P(("groups", "sensor"), None),
    )
    return jax.shard_map(
        per_device,
        mesh=mesh,
        in_specs=placed,
        out_specs=(
            P(("groups", "sensor"), None),
            P(None, ("groups", "sensor")),
            P(None, ("groups", "sensor")),
            P("groups", None),
        ),
        check_vma=False,
    )
```

profile of v0, /device:TPU:0, one launch (start us, length us, event | category | flops | bytes accessed | tf_op | source)
XLA Modules:
  0.0 194.4 jit_solution(2964574075094498716)
XLA Ops:
  8.2 23.4 %all-gather = f32[16,48,12]{1,2,0:T(8,128)S(1)} all-gather(f32[1,48,12]{1,2,0:T(8,128)S(1)} %bitcast.98), channel_id=1, replica_groups=mesh['groups'=2,'sensor'=16] {'sensor'}, dimensions={0}, use_global_device_ids=true | all-gather | bytes 39168 | tf_op jit(solution)/shard_map/all_gather | solution.py:124
  31.8 18.0 %all-gather.1 = f32[16,48,10]{1,2,0:T(8,128)S(1)} all-gather(f32[1,48,10]{1,2,0:T(8,128)} %bitcast.100), channel_id=1, replica_groups=mesh['groups'=2,'sensor'=16] {'sensor'}, dimensions={0}, use_global_device_ids=true | all-gather | bytes 32640 | tf_op jit(solution)/shard_map/all_gather | solution.py:125
  50.0 2.7 %while.88 = (s32[]{:T(128)}, f32[12,48]{1,0:T(8,128)S(1)}, f32[10,768]{1,0:T(8,128)S(1)}, f32[12,768]{1,0:T(8,128)S(1)}, s32[48]{0:T(128)}, /*index=5*/f32[10,76...) while((s32[]{:T(128)}, f32[12,48]{1,0:T(8,128)S(1)}, f32[10,768]{1,0:T(8,128)S(1)}, ...), condition=%wide.region_1.0_spmd.clone, body=%wide.region_0.0_spmd.clone.sunk | while | flops 1783175 | bytes 62065 | solution.py:79
  50.0 0.8 convolution_add_fusion.10
  50.9 0.8 convolution_add_fusion.10
  51.9 0.8 convolution_add_fusion.10
  52.7 1.8 while.89
  52.8 0.3 fusion.128
  53.4 0.3 fusion.128
  53.9 0.3 fusion.128
  54.7 0.3 convolution_convert_fusion.1
  55.3 7.5 %while.87 = (s32[]{:T(128)}, f32[3,256,384]{2,1,0:T(8,128)}, s32[3]{0:T(128)S(1)}, f32[10,768]{1,0:T(8,128)S(1)}, f32[10,48]{1,0:T(8,128)S(1)}, /*index=5*/f32[4...) while((s32[]{:T(128)}, f32[3,256,384]{2,1,0:T(8,128)}, ...), condition=%wide.region_11.12_spmd, body=%wide.region_10.11_spmd.sunk | while | flops 10960902 | bytes 505023 | solution.py:200
  55.3 0.6 dynamic_slice.136
  56.5 0.3 fusion.123
  56.8 1.0 fusion.124
  57.8 0.6 dynamic_slice.136
  59.0 0.3 fusion.123
  59.3 1.0 fusion.124
  60.3 0.6 dynamic_slice.136
  61.5 0.3 fusion.123
  61.8 1.0 fusion.124
  62.9 0.6 copy-done.6
  64.2 0.3 copy-done.5
  64.6 0.2 fusion.62
  65.1 20.4 %all_gather.16 = bf16[768,384]{1,0:T(8,128)(2,1)S(1)} all-gather(bf16[48,384]{1,0:T(8,128)(2,1)S(1)} %reshape.86), channel_id=1, replica_groups=mesh['groups'=2,'sensor'=16] {'sensor'}, dimensions={0}, use_global_device_ids=true | all-gather | bytes 626688 | tf_op jit(solution)/shard_map/all_gather | solution.py:162
  85.5 1.4 while.90
  85.5 0.3 fusion.135
  86.0 0.3 fusion.135
  86.4 0.3 fusion.135
  86.9 0.3 fusion.49
  87.7 20.1 %all_gather.17 = bf16[768,384]{1,0:T(8,128)(2,1)S(1)} all-gather(bf16[48,384]{1,0:T(8,128)(2,1)S(1)} %convert_element_type.68), channel_id=1, replica_groups=mesh['groups'=2,'sensor'=16] {'sensor'}, dimensions={0}, use_global_device_ids=true | all-gather | bytes 626688 | tf_op jit(solution)/shard_map/all_gather | solution.py:176
  107.9 1.4 while.91
  107.9 0.3 fusion.140
  108.3 0.3 fusion.140
  108.8 0.3 fusion.140
  109.2 12.6 %reduce-scatter.5.cloned.1.call-done = f32[48,384]{1,0:T(8,128)} async-done(((f32[768,384]{1,0:T(8,128)}), f32[48,384]{1,0:T(8,128)}) %reduce-scatter.5.cloned.1.call-update) | async-done | bytes 73744 | tf_op jit(solution)/shard_map/reduce_scatter | solution.py:199
  121.9 1.0 add_reduce_fusion
  123.2 3.0 %while.92 = (s32[]{:T(128)}, f32[10,48]{1,0:T(8,128)S(1)}, f32[10,768]{1,0:T(8,128)S(1)}, f32[10,768]{1,0:T(8,128)S(1)}, f32[10,48]{1,0:T(8,128)S(1)}, /*index=5...) while((s32[]{:T(128)}, f32[10,48]{1,0:T(8,128)S(1)}, ...), condition=%wide.region_15.16_spmd.clone, body=%wide.region_14.15_spmd.clone.sunk | while | flops 23399876 | bytes 904809 | solution.py:79
  123.4 0.2 fusion.152
  123.7 0.2 fusion.153
  124.4 0.2 fusion.152
  124.7 0.2 fusion.153
  125.4 0.2 fusion.152
  126.2 0.9 copy.46
  127.2 0.2 fusion.55
  127.7 0.8 reshape.89
  128.5 57.7 %psum.7 = f32[96,32]{0,1:T(8,128)} all-reduce(f32[96,32]{0,1:T(8,128)S(1)} %fusion.55), channel_id=1, replica_groups=mesh['groups'=2,'sensor'=16] {'sensor'}, use_global_device_ids=true, to_apply=%region_17.18 | all-reduce | flops 3072 | bytes 24576 | tf_op jit(solution)/shard_map/psum | solution.py:233
  186.1 1.4 copy.47
  (91 shorter events, 6.9 us)
Async XLA Ops:
  7.2 0.9 copy-start
  7.2 45.6 %copy-start.1 = (f32[10,48]{1,0:T(8,128)S(1)}, f32[10,48]{1,0:T(8,128)}, u32[]{:S(2)}) copy-start(f32[10,48]{1,0:T(8,128)} %param.24) | copy-start | bytes 5764
  7.2 114.7 %reduce-scatter.5.cloned.1.call-start = ((), (), s32[]{:S(2)}) async-start(), calls=%async_computation.2 | async-start | bytes 1253376 | tf_op jit(solution)/shard_map/reduce_scatter | solution.py:199
  31.7 22.8 %copy-start.3 = (bf16[48,384]{1,0:T(8,128)(2,1)S(1)}, bf16[48,384]{1,0:T(8,128)(2,1)}, u32[]{:S(2)}) copy-start(bf16[48,384]{1,0:T(8,128)(2,1)} %param.29) | copy-start | bytes 110596
  31.8 22.9 %copy-start.4 = (bf16[96,32]{0,1:T(8,128)(2,1)S(1)}, bf16[96,32]{0,1:T(8,128)(2,1)}, u32[]{:S(2)}) copy-start(bf16[96,32]{0,1:T(8,128)(2,1)} %param.28) | copy-start | bytes 18436
  62.8 0.7 copy-start.6
  62.8 123.3 %reduce-scatter.7.cloned.1.call-start = ((), (), s32[]{:S(2)}) async-start(), calls=%async_computation.3 | async-start | bytes 417792
  63.8 0.7 copy-start.5
  126.2 61.3 %copy-start.2 = (f32[10,48]{1,0:T(8,128)}, f32[10,48]{1,0:T(8,128)S(1)}, u32[]{:S(2)}) copy-start(f32[10,48]{1,0:T(8,128)S(1)} %get-tuple-element.696) | copy-start | bytes 5764
Sparse Core Ops, SparseCore 0:
  62.9 58.8 reduce-scatter.4
  127.3 54.7 reduce-scatter.6
where the time goes:
time: 195 us; the launch traced here: 194 us
  blocking collectives  140 us (72%)
  between operations  15 us (8%)
  matrix products  13.9 us (7%)
  waiting for transfers between devices  12.7 us (7%)
  local copies, waits for them, and re-layouts  8.47 us (4%)
  loops' own time  2.58 us (1%)
  other arithmetic  2.1 us (1%)
    psum x1, blocking collectives, per_device(): grad_mix = lax.psum(mix_part, 'sensor')  57.7 us
    all_gather x1, blocking collectives, per_device(): lax.all_gather(flat_windows, 'sensor', axis=1, tiled=True)  23.4 us
    all_gather x1, blocking collectives, per_device(): lax.all_gather(hidden, 'sensor', axis=0, tiled=True)  20.4 us
    all_gather x1, blocking collectives, per_device(): lax.all_gather(diffused, 'sensor', axis=0, tiled=True)  20.1 us
    all_gather x1, blocking collectives, per_device(): lax.all_gather(emb_dst, 'sensor', axis=1, tiled=True)  18 us
    reduce_scatter x1, waiting for transfers between devices, per_device(): lax.psum_scatter(lax.map(piece_term, jnp.arange(lax.axis_size('sensor') *...  12.6 us
  transfers between devices with their start and end apart: 2, of which 1 were waited for; matrix products, arithmetic and copies ran while one was open for 3% of the time, Pallas kernels for 0%

commit v1 on v0

--- a/solution.py
+++ b/solution.py
@@ -114,16 +114,45 @@
         )
         return (readings_sum, lax.dynamic_update_slice_in_dim(dst_all, block_dst, offset, 1))
 
+    def _proceed_wall(local):
+        axis_key = "sensor"
+        state_next = lax.psum(1, axis_key)
+        outcome_arr, piece_out, work_now = (state_next, lax.axis_index(axis_key), local.shape[1])
+        passed = lax.dynamic_update_slice_in_dim(
+            jnp.zeros(
+                [u * outcome_arr if tick == 1 else u for tick, u in enumerate(local.shape)],
+                local.dtype,
+            ),
+            local,
+            piece_out * work_now,
+            axis=1,
+        )
+        u1 = h_now = local
+        for dev_i in range(1, outcome_arr // 2 + 1):
+            last = range(outcome_arr)
+            v1 = map(lambda tick: (tick, (tick + 1) % outcome_arr), last)
+            u_next = list(v1)
+            u1 = lax.ppermute(u1, axis_key, u_next)
+            passed = lax.dynamic_update_slice_in_dim(
+                passed, u1, (piece_out - dev_i) % outcome_arr * work_now, axis=1
+            )
+            if 2 * dev_i < outcome_arr:
+                formed = list(
+                    map(lambda tick: (tick, (tick - 1) % outcome_arr), range(outcome_arr))
+                )
+                h_now = lax.ppermute(h_now, axis_key, formed)
+                passed = lax.dynamic_update_slice_in_dim(
+                    passed, h_now, (piece_out + dev_i) % outcome_arr * work_now, axis=1
+                )
+        return passed
+
     readings_sum, dst_all = in_blocks(
         pick_step,
         (
             jnp.zeros((window_rows, local_rows), jnp.float32),
             jnp.zeros((embed_dim, all_rows), jnp.float32),
         ),
-        (
-            lax.all_gather(flat_windows, "sensor", axis=1, tiled=True),
-            lax.all_gather(emb_dst, "sensor", axis=1, tiled=True),
-        ),
+        (_proceed_wall(flat_windows), lax.all_gather(emb_dst, "sensor", axis=1, tiled=True)),
         1,
     )
     readings = readings_sum.T.reshape(local_rows, -1, STEPS)

time: 195 us -> 217 us (1.11)
  starting transfers between devices: 0.08 us -> 28.1 us
  blocking collectives: 140 us -> 118 us
  waiting for transfers between devices: 12.7 us -> 22.9 us
  local copies, waits for them, and re-layouts: 8.47 us -> 14.2 us
    ppermute x0 -> x15, starting transfers between devices: none -> 28 us  [the longest x7 27.1 us: _proceed_wall(): h_now = lax.ppermute(h_now, axis_key, formed)]
    all_gather x1 -> x0, blocking collectives: 23.4 us -> none  [per_device(): lax.all_gather(flat_windows, 'sensor', axis=1, tiled=True)]
    ppermute x0 -> x15, waiting for transfers between devices: none -> 6.51 us  [the longest x7 6.05 us: _proceed_wall(): h_now = lax.ppermute(h_now, axis_key, formed)]
    dynamic_update_slice x0 -> x16, local copies, waits for them, and re-layouts: none -> 4.95 us  [the longest x8 2.4 us: _proceed_wall(): lax.dynamic_update_slice_in_dim(passed, u1, (piece_out - dev_i) % outcome...]
    reduce_scatter x1, waiting for transfers between devices: 12.6 us -> 16.3 us  [per_device(): lax.psum_scatter(lax.map(piece_term, jnp.arange(lax.axis_size('sensor') *...]
  transfers between devices with their start and end apart: 2 -> 17, of which waited for: 1 -> 12; matrix products, arithmetic and copies ran while one was open for 3% -> 7% of each run, Pallas kernels for 0% -> 0%
where the time goes in v1:
time: 217 us
  blocking collectives  118 us (54%)
  starting transfers between devices  28.1 us (13%)
  waiting for transfers between devices  22.9 us (11%)
  between operations  15.1 us (7%)
  local copies, waits for them, and re-layouts  14.2 us (7%)
  matrix products  13.3 us (6%)
  loops' own time  2.51 us (1%)
    psum x1, blocking collectives, per_device(): grad_mix = lax.psum(mix_part, 'sensor')  57.7 us
    ppermute x7, starting transfers between devices, _proceed_wall(): h_now = lax.ppermute(h_now, axis_key, formed)  27.1 us
    all_gather x1, blocking collectives, per_device(): lax.all_gather(diffused, 'sensor', axis=0, tiled=True)  21.1 us
    all_gather x1, blocking collectives, per_device(): lax.all_gather(emb_dst, 'sensor', axis=1, tiled=True)  19.9 us
    all_gather x1, blocking collectives, per_device(): lax.all_gather(hidden, 'sensor', axis=0, tiled=True)  19.6 us
    reduce_scatter x1, waiting for transfers between devices, per_device(): lax.psum_scatter(lax.map(piece_term, jnp.arange(lax.axis_size('sensor') *...  16.3 us
    ppermute x7, waiting for transfers between devices, _proceed_wall(): h_now = lax.ppermute(h_now, axis_key, formed)  6.05 us
  transfers between devices with their start and end apart: 17, of which 12 were waited for; matrix products, arithmetic and copies ran while one was open for 7% of the time, Pallas kernels for 0%

profile of v1, /device:TPU:0, one launch (start us, length us, event | category | flops | bytes accessed | tf_op | source)
XLA Modules:
  0.0 216.5 jit_solution(15011983800272006375)
XLA Ops:
  8.2 0.5 collective-permute-start
  8.7 5.0 %collective-permute-start.1 = (f32[12,48]{1,0:T(8,128)S(1)}, f32[12,48]{1,0:T(8,128)S(1)}, u32[]{:S(2)}, u32[]{:S(2)}) collective-permute-start(f32[12,48]{1,0:T(8,128)S(1)} %copy.47), channel_id=1, source_target_pairs={{0,15},{1,0},{2,1},{3,2},{4,3},{5,4},{6,5},{7,6},{8,7},{9,8},{10,9... | collective-permute-start | bytes 6920 | tf_op jit(solution)/shard_map/ppermute | solution.py:143
  13.7 0.9 reshape.90
  14.6 1.0 convolution_convert_fusion.1
  15.6 1.0 fusion.49
  16.6 0.8 slice_bitcast_fusion.1
  17.3 19.9 %all-gather = f32[16,48,10]{1,2,0:T(8,128)S(1)} all-gather(f32[1,48,10]{1,2,0:T(8,128)} %bitcast.92), channel_id=1, replica_groups=mesh['groups'=2,'sensor'=16] {'sensor'}, dimensions={0}, use_global_device_ids=true | all-gather | bytes 32640 | tf_op jit(solution)/shard_map/all_gather | solution.py:155
  37.3 0.5 collective-permute-start.4
  37.8 0.9 collective-permute-done.3
  38.7 4.4 %collective-permute-start.5 = (f32[12,48]{1,0:T(8,128)S(1)}, f32[12,48]{1,0:T(8,128)S(1)}, u32[]{:S(2)}, u32[]{:S(2)}) collective-permute-start(f32[12,48]{1,0:T(8,128)S(1)} %collective-permute-done.3), channel_id=1, source_target_pairs={{0,15},{1,0},{2,1},{3,2},{4,3},{5,4},{6,5},{7,6},{8,7},{9,8},{10,9... | collective-permute-start | bytes 6920 | tf_op jit(solution)/shard_map/ppermute | solution.py:143
  43.1 1.3 collective-permute-done.5
  44.4 4.4 %collective-permute-start.7 = (f32[12,48]{1,0:T(8,128)S(1)}, f32[12,48]{1,0:T(8,128)S(1)}, u32[]{:S(2)}, u32[]{:S(2)}) collective-permute-start(f32[12,48]{1,0:T(8,128)S(1)} %collective-permute-done.5), channel_id=1, source_target_pairs={{0,15},{1,0},{2,1},{3,2},{4,3},{5,4},{6,5},{7,6},{8,7},{9,8},{10,9... | collective-permute-start | bytes 6920 | tf_op jit(solution)/shard_map/ppermute | solution.py:143
  48.9 1.3 collective-permute-done.7
  50.2 4.4 %collective-permute-start.9 = (f32[12,48]{1,0:T(8,128)S(1)}, f32[12,48]{1,0:T(8,128)S(1)}, u32[]{:S(2)}, u32[]{:S(2)}) collective-permute-start(f32[12,48]{1,0:T(8,128)S(1)} %collective-permute-done.7), channel_id=1, source_target_pairs={{0,15},{1,0},{2,1},{3,2},{4,3},{5,4},{6,5},{7,6},{8,7},{9,8},{10,9... | collective-permute-start | bytes 6920 | tf_op jit(solution)/shard_map/ppermute | solution.py:143
  54.7 1.3 collective-permute-done.9
  56.0 4.4 %collective-permute-start.11 = (f32[12,48]{1,0:T(8,128)S(1)}, f32[12,48]{1,0:T(8,128)S(1)}, u32[]{:S(2)}, u32[]{:S(2)}) collective-permute-start(f32[12,48]{1,0:T(8,128)S(1)} %collective-permute-done.9), channel_id=1, source_target_pairs={{0,15},{1,0},{2,1},{3,2},{4,3},{5,4},{6,5},{7,6},{8,7},{9,8},{10,9... | collective-permute-start | bytes 6920 | tf_op jit(solution)/shard_map/ppermute | solution.py:143
  60.5 1.3 collective-permute-done.11
  61.8 4.4 %collective-permute-start.13 = (f32[12,48]{1,0:T(8,128)S(1)}, f32[12,48]{1,0:T(8,128)S(1)}, u32[]{:S(2)}, u32[]{:S(2)}) collective-permute-start(f32[12,48]{1,0:T(8,128)S(1)} %collective-permute-done.11), channel_id=1, source_target_pairs={{0,15},{1,0},{2,1},{3,2},{4,3},{5,4},{6,5},{7,6},{8,7},{9,8},{10,9... | collective-permute-start | bytes 6920 | tf_op jit(solution)/shard_map/ppermute | solution.py:143
  68.5 0.3 dynamic_update_slice.71
  68.9 0.3 dynamic_update_slice.72
  69.2 0.3 dynamic_update_slice.73
  69.5 0.3 dynamic_update_slice.74
  69.9 0.3 dynamic_update_slice.75
  70.5 0.3 dynamic_update_slice.77
  71.5 0.3 dynamic_update_slice.80
  72.2 0.8 while.88
  73.0 1.8 while.89
  73.0 0.3 fusion.128
  73.6 0.3 fusion.128
  74.2 0.3 fusion.128
  74.8 7.5 %while.87 = (s32[]{:T(128)}, f32[3,256,384]{2,1,0:T(8,128)}, s32[3]{0:T(128)S(1)}, f32[10,768]{1,0:T(8,128)S(1)}, f32[10,48]{1,0:T(8,128)S(1)}, /*index=5*/f32[4...) while((s32[]{:T(128)}, f32[3,256,384]{2,1,0:T(8,128)}, ...), condition=%wide.region_11.12_spmd, body=%wide.region_10.11_spmd.sunk | while | flops 10960902 | bytes 505523 | solution.py:229
  74.8 0.6 dynamic_slice.136
  76.3 1.0 fusion.124
  77.3 0.6 dynamic_slice.136
  78.8 1.0 fusion.124
  79.7 0.6 dynamic_slice.136
  81.2 1.0 fusion.124
  83.7 19.6 %all_gather.12 = bf16[768,384]{1,0:T(8,128)(2,1)S(1)} all-gather(bf16[48,384]{1,0:T(8,128)(2,1)S(1)} %reshape.86), channel_id=1, replica_groups=mesh['groups'=2,'sensor'=16] {'sensor'}, dimensions={0}, use_global_device_ids=true | all-gather | bytes 626688 | tf_op jit(solution)/shard_map/all_gather | solution.py:191
  103.3 1.4 while.90
  105.2 21.1 %all_gather.13 = bf16[768,384]{1,0:T(8,128)(2,1)S(1)} all-gather(bf16[48,384]{1,0:T(8,128)(2,1)S(1)} %convert_element_type.68), channel_id=1, replica_groups=mesh['groups'=2,'sensor'=16] {'sensor'}, dimensions={0}, use_global_device_ids=true | all-gather | bytes 626688 | tf_op jit(solution)/shard_map/all_gather | solution.py:205
  126.3 1.4 while.91
  127.7 16.3 %reduce-scatter.5.cloned.1.call-done = f32[48,384]{1,0:T(8,128)} async-done(((f32[768,384]{1,0:T(8,128)}), f32[48,384]{1,0:T(8,128)}) %reduce-scatter.5.cloned.1.call-update) | async-done | bytes 73744 | tf_op jit(solution)/shard_map/reduce_scatter | solution.py:228
  144.0 1.0 add_reduce_fusion
  145.3 3.0 %while.92 = (s32[]{:T(128)}, f32[10,48]{1,0:T(8,128)S(1)}, f32[10,768]{1,0:T(8,128)S(1)}, f32[10,768]{1,0:T(8,128)S(1)}, f32[10,48]{1,0:T(8,128)S(1)}, /*index=5...) while((s32[]{:T(128)}, f32[10,48]{1,0:T(8,128)S(1)}, ...), condition=%wide.region_15.16_spmd.clone, body=%wide.region_14.15_spmd.clone.sunk | while | flops 23399876 | bytes 904801 | solution.py:79
  148.3 0.9 copy.45
  149.8 0.8 reshape.89
  150.6 57.7 %psum.7 = f32[96,32]{0,1:T(8,128)} all-reduce(f32[96,32]{0,1:T(8,128)S(1)} %fusion.55), channel_id=1, replica_groups=mesh['groups'=2,'sensor'=16] {'sensor'}, use_global_device_ids=true, to_apply=%region_17.18 | all-reduce | flops 3072 | bytes 24576 | tf_op jit(solution)/shard_map/psum | solution.py:262
  208.3 1.4 copy.46
  (133 shorter events, 14.3 us)
Async XLA Ops:
  7.2 0.9 copy-start
  7.2 136.8 %reduce-scatter.5.cloned.1.call-start = ((), (), s32[]{:S(2)}) async-start(), calls=%async_computation.2 | async-start | bytes 1253376 | tf_op jit(solution)/shard_map/reduce_scatter | solution.py:228
  8.2 9.1 %collective-permute-start = (f32[12,48]{1,0:T(8,128)S(1)}, f32[12,48]{1,0:T(8,128)S(1)}, u32[]{:S(2)}, u32[]{:S(2)}) collective-permute-start(f32[12,48]{1,0:T(8,128)S(1)} %copy.47), channel_id=1, source_target_pairs={{0,1},{1,2},{2,3},{3,4},{4,5},{5,6},{6,7},{7,8},{8,9},{9,10},{10,1... | collective-permute-start | bytes 6920 | tf_op jit(solution)/shard_map/ppermute | solution.py:135
  8.7 28.6 %collective-permute-start.1 = (f32[12,48]{1,0:T(8,128)S(1)}, f32[12,48]{1,0:T(8,128)S(1)}, u32[]{:S(2)}, u32[]{:S(2)}) collective-permute-start(f32[12,48]{1,0:T(8,128)S(1)} %copy.47), channel_id=1, source_target_pairs={{0,15},{1,0},{2,1},{3,2},{4,3},{5,4},{6,5},{7,6},{8,7},{9,8},{10,9... | collective-permute-start | bytes 6920 | tf_op jit(solution)/shard_map/ppermute | solution.py:143
  17.3 20.0 %collective-permute-start.2 = (f32[12,48]{1,0:T(8,128)S(1)}, f32[12,48]{1,0:T(8,128)S(1)}, u32[]{:S(2)}, u32[]{:S(2)}) collective-permute-start(f32[12,48]{1,0:T(8,128)S(1)} %collective-permute-done), channel_id=1, source_target_pairs={{0,1},{1,2},{2,3},{3,4},{4,5},{5,6},{6,7},{7,8},{8,9},{9,10},{10,1... | collective-permute-start | bytes 6920 | tf_op jit(solution)/shard_map/ppermute | solution.py:135
  37.3 34.9 %copy-start.5 = (s32[48]{0:T(128)S(1)}, s32[48]{0:T(128)}, u32[]{:S(2)}) copy-start(s32[48]{0:T(128)} %param.23) | copy-start | bytes 580
  37.3 1.4 collective-permute-start.3
  37.3 5.8 %collective-permute-start.4 = (f32[12,48]{1,0:T(8,128)S(1)}, f32[12,48]{1,0:T(8,128)S(1)}, u32[]{:S(2)}, u32[]{:S(2)}) collective-permute-start(f32[12,48]{1,0:T(8,128)S(1)} %collective-permute-done.2), channel_id=1, source_target_pairs={{0,1},{1,2},{2,3},{3,4},{4,5},{5,6},{6,7},{7,8},{8,9},{9,10},{10,1... | collective-permute-start | bytes 6920 | tf_op jit(solution)/shard_map/ppermute | solution.py:135
  38.7 5.8 %collective-permute-start.5 = (f32[12,48]{1,0:T(8,128)S(1)}, f32[12,48]{1,0:T(8,128)S(1)}, u32[]{:S(2)}, u32[]{:S(2)}) collective-permute-start(f32[12,48]{1,0:T(8,128)S(1)} %collective-permute-done.3), channel_id=1, source_target_pairs={{0,15},{1,0},{2,1},{3,2},{4,3},{5,4},{6,5},{7,6},{8,7},{9,8},{10,9... | collective-permute-start | bytes 6920 | tf_op jit(solution)/shard_map/ppermute | solution.py:143
  43.1 5.8 %collective-permute-start.6 = (f32[12,48]{1,0:T(8,128)S(1)}, f32[12,48]{1,0:T(8,128)S(1)}, u32[]{:S(2)}, u32[]{:S(2)}) collective-permute-start(f32[12,48]{1,0:T(8,128)S(1)} %collective-permute-done.4), channel_id=1, source_target_pairs={{0,1},{1,2},{2,3},{3,4},{4,5},{5,6},{6,7},{7,8},{8,9},{9,10},{10,1... | collective-permute-start | bytes 6920 | tf_op jit(solution)/shard_map/ppermute | solution.py:135
  44.4 5.8 %collective-permute-start.7 = (f32[12,48]{1,0:T(8,128)S(1)}, f32[12,48]{1,0:T(8,128)S(1)}, u32[]{:S(2)}, u32[]{:S(2)}) collective-permute-start(f32[12,48]{1,0:T(8,128)S(1)} %collective-permute-done.5), channel_id=1, source_target_pairs={{0,15},{1,0},{2,1},{3,2},{4,3},{5,4},{6,5},{7,6},{8,7},{9,8},{10,9... | collective-permute-start | bytes 6920 | tf_op jit(solution)/shard_map/ppermute | solution.py:143
  48.9 5.8 %collective-permute-start.8 = (f32[12,48]{1,0:T(8,128)S(1)}, f32[12,48]{1,0:T(8,128)S(1)}, u32[]{:S(2)}, u32[]{:S(2)}) collective-permute-start(f32[12,48]{1,0:T(8,128)S(1)} %collective-permute-done.6), channel_id=1, source_target_pairs={{0,1},{1,2},{2,3},{3,4},{4,5},{5,6},{6,7},{7,8},{8,9},{9,10},{10,1... | collective-permute-start | bytes 6920 | tf_op jit(solution)/shard_map/ppermute | solution.py:135
  50.2 5.8 %collective-permute-start.9 = (f32[12,48]{1,0:T(8,128)S(1)}, f32[12,48]{1,0:T(8,128)S(1)}, u32[]{:S(2)}, u32[]{:S(2)}) collective-permute-start(f32[12,48]{1,0:T(8,128)S(1)} %collective-permute-done.7), channel_id=1, source_target_pairs={{0,15},{1,0},{2,1},{3,2},{4,3},{5,4},{6,5},{7,6},{8,7},{9,8},{10,9... | collective-permute-start | bytes 6920 | tf_op jit(solution)/shard_map/ppermute | solution.py:143
  54.7 5.8 %collective-permute-start.10 = (f32[12,48]{1,0:T(8,128)S(1)}, f32[12,48]{1,0:T(8,128)S(1)}, u32[]{:S(2)}, u32[]{:S(2)}) collective-permute-start(f32[12,48]{1,0:T(8,128)S(1)} %collective-permute-done.8), channel_id=1, source_target_pairs={{0,1},{1,2},{2,3},{3,4},{4,5},{5,6},{6,7},{7,8},{8,9},{9,10},{10,1... | collective-permute-start | bytes 6920 | tf_op jit(solution)/shard_map/ppermute | solution.py:135
  56.0 5.8 %collective-permute-start.11 = (f32[12,48]{1,0:T(8,128)S(1)}, f32[12,48]{1,0:T(8,128)S(1)}, u32[]{:S(2)}, u32[]{:S(2)}) collective-permute-start(f32[12,48]{1,0:T(8,128)S(1)} %collective-permute-done.9), channel_id=1, source_target_pairs={{0,15},{1,0},{2,1},{3,2},{4,3},{5,4},{6,5},{7,6},{8,7},{9,8},{10,9... | collective-permute-start | bytes 6920 | tf_op jit(solution)/shard_map/ppermute | solution.py:143
  60.5 5.8 %collective-permute-start.12 = (f32[12,48]{1,0:T(8,128)S(1)}, f32[12,48]{1,0:T(8,128)S(1)}, u32[]{:S(2)}, u32[]{:S(2)}) collective-permute-start(f32[12,48]{1,0:T(8,128)S(1)} %collective-permute-done.10), channel_id=1, source_target_pairs={{0,1},{1,2},{2,3},{3,4},{4,5},{5,6},{6,7},{7,8},{8,9},{9,10},{10,1... | collective-permute-start | bytes 6920 | tf_op jit(solution)/shard_map/ppermute | solution.py:135
  61.8 9.8 %collective-permute-start.13 = (f32[12,48]{1,0:T(8,128)S(1)}, f32[12,48]{1,0:T(8,128)S(1)}, u32[]{:S(2)}, u32[]{:S(2)}) collective-permute-start(f32[12,48]{1,0:T(8,128)S(1)} %collective-permute-done.11), channel_id=1, source_target_pairs={{0,15},{1,0},{2,1},{3,2},{4,3},{5,4},{6,5},{7,6},{8,7},{9,8},{10,9... | collective-permute-start | bytes 6920 | tf_op jit(solution)/shard_map/ppermute | solution.py:143
  66.2 5.8 %collective-permute-start.14 = (f32[12,48]{1,0:T(8,128)S(1)}, f32[12,48]{1,0:T(8,128)S(1)}, u32[]{:S(2)}, u32[]{:S(2)}) collective-permute-start(f32[12,48]{1,0:T(8,128)S(1)} %collective-permute-done.12), channel_id=1, source_target_pairs={{0,1},{1,2},{2,3},{3,4},{4,5},{5,6},{6,7},{7,8},{8,9},{9,10},{10,1... | collective-permute-start | bytes 6920 | tf_op jit(solution)/shard_map/ppermute | solution.py:135
  66.3 6.7 %copy-start.1 = (f32[10,48]{1,0:T(8,128)S(1)}, f32[10,48]{1,0:T(8,128)}, u32[]{:S(2)}) copy-start(f32[10,48]{1,0:T(8,128)} %param.24) | copy-start | bytes 5764
  82.3 126.0 %reduce-scatter.7.cloned.1.call-start = ((), (), s32[]{:S(2)}) async-start(), calls=%async_computation.3 | async-start | bytes 417792
  82.4 0.7 copy-start.4
  148.3 61.4 %copy-start.2 = (f32[10,48]{1,0:T(8,128)}, f32[10,48]{1,0:T(8,128)S(1)}, u32[]{:S(2)}) copy-start(f32[10,48]{1,0:T(8,128)S(1)} %get-tuple-element.696) | copy-start | bytes 5764
  148.3 1.2 copy-start.3
Sparse Core Ops, SparseCore 0:
  82.4 61.5 reduce-scatter.4
  149.4 54.6 reduce-scatter.6
